TPU v7x, 32 devices: a whole 2x2x4 slice. The times are simulated.
32 devices in a mesh: groups: 2 (over x), branch: 16 (over z, y, core).
Axes of the slice: x: 2, y: 2, z: 4, core: 2. Of those that a mesh axis runs over, the one named last changes fastest.
Arguments:
- prompt_k: bfloat16 [32, 1024, 1024], P(('groups', 'branch')), parts along dimension 0, may hold values from -6 to 6
- prompt_v: bfloat16 [32, 1024, 1024], P(('groups', 'branch')), parts along dimension 0, may hold values from -6 to 6
- prompt_mask: int32 [32, 8], P(('groups', 'branch')), parts along dimension 0, may hold values from 0 to 1, as said below
- shared_kv: bfloat16 [64, 24, 2048], P(('groups', 'branch')), parts along dimension 0, may hold values from -6 to 6
- shared_len: int32 [64], P(('groups', 'branch')), parts along dimension 0, may hold values from 1 to 24, 400 in all
- send_pick: int32 [32, 16], P(('groups', 'branch')), parts along dimension 0, may hold values from -1 to 1, as said below
- unique_q: bfloat16 [512, 8192], P(('groups', 'branch')), parts along dimension 0, may hold values from -132 to 132
- unique_kv: bfloat16 [512, 2048], P(('groups', 'branch')), parts along dimension 0, may hold values from -6.5 to 6.5
- unique_owner: int32 [512, 1], P(('groups', 'branch')), parts along dimension 0, may hold values from 0 to 15; in each aligned block of 16 rows (0 to 15, 16 to 31, ...) at most 2 rows name the same one
Outputs:
- attended: bfloat16 [512, 8192], P(('groups', 'branch')), parts along dimension 0
There are 2 independent parts, one for each index of `groups`. A program takes and returns all parts, laid end to end along the dimension named above; each array names one. Nothing has to cross between parts.
Inputs may be any that keep to these rules, and one draw needn't show every extreme that they name: `prompt_mask`: block 0 of every branch's prompt is visible. `send_pick`: entry [s, b] names which of owner s's 2 results branch b subscribes to, or -1 for none; every branch subscribes to exactly 12 results, at most one of each owner. `unique_owner`: among the rows of one source, no branch is named by more than 2 rows.
All inputs are finite; a program needn't handle non-finite values. No bound on the sum of `shared_len` on one device may be relied on, other than what follows from the above.
Results may differ from a plain program's by a relative error of at most 0.0027.
Values may be sent and summed in bfloat16 or wider, within the bound.
A program may use at most 128 MiB of HBM per device.

v0:
```python
import math

import jax
import jax.numpy as jnp
from jax import lax
from jax.sharding import PartitionSpec as P

QH = 64
KVH = 8
HD = 128
GRP = 8


def attend(queries, key_rows, value_rows, allowed):
    count = queries.shape[0]
    keys_total = key_rows.shape[0]
    grouped = queries.reshape(count, KVH, GRP, HD).transpose(1, 2, 0, 3)
    key_heads = key_rows.reshape(keys_total, KVH, HD).transpose(1, 0, 2)
    value_heads = value_rows.reshape(keys_total, KVH, HD).transpose(1, 0, 2)
    scale = 1.0 / math.sqrt(HD)

    def one_head(operands):
        query_group, key_group, value_group = operands
        scores = (
            jnp.einsum("gsd,kd->gsk", query_group, key_group, preferred_element_type=jnp.float32)
            * scale
        )
        scores = jnp.where(allowed[None], scores, -1e30)
        largest = jnp.max(scores, axis=-1, keepdims=True)
        weights = jnp.exp(scores - largest)
        total = jnp.sum(weights, axis=-1, keepdims=True)
        probs = weights.astype(jnp.bfloat16)
        mixed = jnp.einsum("gsk,kd->gsd", probs, value_group, preferred_element_type=jnp.float32)
        return (mixed / total).astype(jnp.bfloat16)

    heads = lax.map(one_head, (grouped, key_heads, value_heads))
    return heads.transpose(2, 0, 1, 3).reshape(count, QH * HD)


def select(stack, lengths, picked):
    chosen = jnp.zeros((picked.shape[0],) + stack.shape[2:], jnp.bfloat16)
    live_len = jnp.zeros(picked.shape, jnp.int32)
    for which in range(stack.shape[1]):
        match = picked == which
        chosen = jnp.where(match[:, None, None], stack[:, which], chosen)
        live_len = jnp.where(match, lengths[:, which], live_len)
    return (chosen, live_len)


def body(
    prompt_k,
    prompt_v,
    prompt_mask,
    shared_kv,
    shared_len,
    send_pick,
    unique_q,
    unique_kv,
    unique_owner,
):
    branches = lax.axis_size("branch")
    row_count = unique_q.shape[0]
    capacity = 2 * row_count // branches
    width = branches * capacity
    kv_width = unique_kv.shape[1] // 2
    result_rows = shared_kv.shape[1]
    owner_of = unique_owner[:, 0]
    in_device = jnp.arange(row_count, dtype=jnp.int32)
    earlier = (owner_of[:, None] == owner_of[None, :]) & (in_device[None, :] < in_device[:, None])
    slot_index = owner_of * capacity + jnp.sum(earlier.astype(jnp.int32), axis=1)
    matches = jnp.arange(width, dtype=jnp.int32)[:, None] == slot_index[None, :]
    placing = matches.astype(jnp.bfloat16)
    send_q = (
        jnp.dot(placing, unique_q, preferred_element_type=jnp.float32)
        .astype(jnp.bfloat16)
        .reshape(branches, capacity, -1)
    )
    send_pairs = (
        jnp.dot(placing, unique_kv, preferred_element_type=jnp.float32)
        .astype(jnp.bfloat16)
        .reshape(branches, capacity, -1)
    )
    send_live = jnp.any(matches, axis=1).astype(jnp.int32).reshape(branches, capacity)
    recv_q, recv_pairs, recv_live = (
        lax.all_to_all(send_q, "branch", split_axis=0, concat_axis=0, tiled=True),
        lax.all_to_all(send_pairs, "branch", split_axis=0, concat_axis=0, tiled=True),
        lax.all_to_all(send_live, "branch", split_axis=0, concat_axis=0, tiled=True),
    )
    outgoing, outgoing_len = select(shared_kv[None], shared_len[None], send_pick[0])
    fetched, live_len = (
        lax.all_to_all(outgoing, "branch", split_axis=0, concat_axis=0, tiled=True),
        lax.all_to_all(outgoing_len, "branch", split_axis=0, concat_axis=0, tiled=True),
    )
    queries = recv_q.reshape(width, -1)
    pairs = recv_pairs.reshape(width, -1)
    slot_live = recv_live.reshape(width) > 0
    fetched_rows = fetched.reshape(branches * result_rows, 2 * kv_width)
    shared_ok = (jnp.arange(result_rows, dtype=jnp.int32)[None, :] < live_len[:, None]).reshape(
        branches * result_rows
    )
    block_size = prompt_k.shape[1] // prompt_mask.shape[1]
    block_ok = jnp.repeat(prompt_mask[0] > 0, block_size)
    slot_range = jnp.arange(width, dtype=jnp.int32)
    unique_ok = (slot_range[None, :] <= slot_range[:, None]) & slot_live[None, :]
    allowed = jnp.concatenate(
        [
            jnp.broadcast_to(block_ok[None], (width, block_ok.shape[0])),
            jnp.broadcast_to(shared_ok[None], (width, shared_ok.shape[0])),
            unique_ok,
        ],
        axis=1,
    )
    key_rows = jnp.concatenate(
        [prompt_k[0], fetched_rows[:, :kv_width], pairs[:, :kv_width]], axis=0
    )
    value_rows = jnp.concatenate(
        [prompt_v[0], fetched_rows[:, kv_width:], pairs[:, kv_width:]], axis=0
    )
    outputs = attend(queries, key_rows, value_rows, allowed)
    returned = lax.all_to_all(
        outputs.reshape(branches, capacity, -1), "branch", split_axis=0, concat_axis=0, tiled=True
    )
    return jnp.dot(
        placing.T, returned.reshape(width, -1), preferred_element_type=jnp.float32
    ).astype(jnp.bfloat16)


def solution(mesh):
    in_specs = (
        P(("groups", "branch"), None, None),
        P(("groups", "branch"), None, None),
        P(("groups", "branch"), None),
        P(("groups", "branch"), None, None),
        P(("groups", "branch")),
        P(("groups", "branch"), None),
        P(("groups", "branch"), None),
        P(("groups", "branch"), None),
        P(("groups", "branch"), None),
    )
    out_specs = P(("groups", "branch"), None)
    return jax.shard_map(body, mesh=mesh, in_specs=in_specs, out_specs=out_specs, check_vma=False)
```

profile of v0, /device:TPU:0, one launch (start us, length us, event | category | flops | bytes accessed | tf_op | source)
XLA Modules:
  0.0 170.4 jit_solution(4831581094639258558)
XLA Ops:
  3.9 7.4 %all-to-all-start = ((s32[16,1,1]{2,1,0:T(1,128)}), s32[16,1,1]{2,1,0:T(1,128)S(1)}, u32[]{:S(2)}, u32[]{:S(2)}) async-start(s32[16,1,1]{2,1,0:T(1,128)} %copy.54), calls=%async_computation | async-start | bytes 16384 | tf_op jit(solution)/shard_map/all_to_all | solution.py:92
  13.7 4.0 %all-to-all-done = s32[16,1,1]{2,1,0:T(1,128)S(1)} async-done(((s32[16,1,1]{2,1,0:T(1,128)}), s32[16,1,1]{2,1,0:T(1,128)S(1)}, u32[]{:S(2)}, u32[]{:S(2)}) %all-to-all-start) | async-done | bytes 96 | tf_op jit(solution)/shard_map/all_to_all | solution.py:92
  17.7 3.4 %all-to-all-start.1 = ((s32[16,1,2]{2,1,0:T(1,128)}), s32[16,1,2]{2,1,0:T(1,128)S(1)}, u32[]{:S(2)}, u32[]{:S(2)}) async-start(s32[16,1,2]{2,1,0:T(1,128)} %bitcast.13), calls=%async_computation.1 | async-start | bytes 16384 | tf_op jit(solution)/shard_map/all_to_all | solution.py:87
  23.1 4.5 %all-to-all-done.1 = s32[16,1,2]{2,1,0:T(1,128)S(1)} async-done(((s32[16,1,2]{2,1,0:T(1,128)}), s32[16,1,2]{2,1,0:T(1,128)S(1)}, u32[]{:S(2)}, u32[]{:S(2)}) %all-to-all-start.1) | async-done | bytes 160 | tf_op jit(solution)/shard_map/all_to_all | solution.py:87
  27.6 3.5 %all-to-all-start.4 = ((bf16[16,2,2048]{2,1,0:T(2,128)(2,1)}), bf16[16,2,2048]{2,1,0:T(2,128)(2,1)S(1)}, u32[]{:S(2)}, u32[]{:S(2)}) async-start(bf16[16,2,2048]{2,1,0:T(2,128)(2,1)} %reshape.133), calls=%async_computation.4 | async-start | bytes 262144 | tf_op jit(solution)/shard_map/all_to_all | solution.py:86
  32.6 6.3 %all-to-all-done.4 = bf16[16,2,2048]{2,1,0:T(2,128)(2,1)S(1)} async-done(((bf16[16,2,2048]{2,1,0:T(2,128)(2,1)}), bf16[16,2,2048]{2,1,0:T(2,128)(2,1)S(1)}, u32[]{:S(2)}, u32[]{:S(2)}) %all-to-all-start.4) | async-done | bytes 131104 | tf_op jit(solution)/shard_map/all_to_all | solution.py:86
  39.0 3.6 %all-to-all-start.2 = ((bf16[16,2,8192]{2,1,0:T(2,128)(2,1)}), bf16[16,2,8192]{2,1,0:T(2,128)(2,1)S(1)}, u32[]{:S(2)}, u32[]{:S(2)}) async-start(bf16[16,2,8192]{2,1,0:T(2,128)(2,1)} %reshape.131), calls=%async_computation.2 | async-start | bytes 1048576 | tf_op jit(solution)/shard_map/all_to_all | solution.py:85
  44.0 12.8 %all-to-all-done.2 = bf16[16,2,8192]{2,1,0:T(2,128)(2,1)S(1)} async-done(((bf16[16,2,8192]{2,1,0:T(2,128)(2,1)}), bf16[16,2,8192]{2,1,0:T(2,128)(2,1)S(1)}, u32[]{:S(2)}, u32[]{:S(2)}) %all-to-all-start.2) | async-done | bytes 524320 | tf_op jit(solution)/shard_map/all_to_all | solution.py:85
  56.8 4.1 %all-to-all-start.3 = ((bf16[16,24,2048]{2,1,0:T(8,128)(2,1)}), bf16[16,24,2048]{2,1,0:T(8,128)(2,1)S(1)}, u32[]{:S(2)}, u32[]{:S(2)}) async-start(bf16[16,24,2048]{2,1,0:T(8,128)(2,1)} %select_select_fusion), calls=%async_computation.3 | async-start | bytes 3145728 | tf_op jit(solution)/shard_map/all_to_all | solution.py:91
  60.9 3.9 %copy.56 = bf16[1,1024,1024]{1,2,0:T(8,128)(2,1)} copy(bf16[1,1024,1024]{2,1,0:T(8,128)(2,1)} %param.11) | data formatting | bytes 4194304 | tf_op args[0]
  64.8 4.0 %copy.59 = bf16[1,1024,1024]{1,2,0:T(8,128)(2,1)} copy(bf16[1,1024,1024]{2,1,0:T(8,128)(2,1)} %param.12) | data formatting | bytes 4194304 | tf_op args[1]
  72.5 20.2 %all-to-all-done.3 = bf16[16,24,2048]{2,1,0:T(8,128)(2,1)S(1)} async-done(((bf16[16,24,2048]{2,1,0:T(8,128)(2,1)}), bf16[16,24,2048]{2,1,0:T(8,128)(2,1)S(1)}, u32[]{:S(2)}, u32[]{:S(2)}) %all-to-all-start.3) | async-done | bytes 1572896 | tf_op jit(solution)/shard_map/all_to_all | solution.py:91
  94.9 2.2 %maximum_bitcast_fusion = bf16[8,1440,128]{1,2,0:T(8,128)(2,1)S(1)} fusion(bf16[32,8,128]{0,2,1:T(8,128)(2,1)} %bitcast.73, bf16[384,8,128]{0,2,1:T(8,128)(2,1)} %bitcast.69, bf16[1024,8,128]{0,2,1:T(8,128)(2,1)} %bitcast.67), kind=kLoop, calls=%fused_computation.20 | loop fusion | flops 8847360 | bytes 5898240 | tf_op jit(solution)/shard_map/transpose | solution.py:18
  97.1 2.8 %copy.63 = bf16[8,1440,128]{2,1,0:T(8,128)(2,1)} copy(bf16[8,1440,128]{1,2,0:T(8,128)(2,1)S(1)} %maximum_bitcast_fusion) | data formatting | bytes 5898240 | tf_op jit(solution)/shard_map/while | solution.py:36
  99.9 2.3 %copy.60 = bf16[384,1024]{0,1:T(8,128)(2,1)} copy(bf16[384,1024]{1,0:T(8,128)(2,1)} %get-tuple-element.82) | data formatting | bytes 1572864 | tf_op jit(solution)/shard_map/slice | solution.py:117
  102.2 2.2 %maximum_bitcast_fusion.1 = bf16[8,1440,128]{1,2,0:T(8,128)(2,1)S(1)} fusion(bf16[32,8,128]{0,2,1:T(8,128)(2,1)} %bitcast.72, bf16[384,8,128]{0,2,1:T(8,128)(2,1)} %bitcast.70, bf16[1024,8,128]{0,2,1:T(8,128)(2,1)} %bitcast.66), kind=kLoop, calls=%fused_computation.21 | loop fusion | flops 8847360 | bytes 5898240 | tf_op jit(solution)/shard_map/transpose | solution.py:19
  104.4 2.8 %copy.64 = bf16[8,1440,128]{2,1,0:T(8,128)(2,1)} copy(bf16[8,1440,128]{1,2,0:T(8,128)(2,1)S(1)} %maximum_bitcast_fusion.1) | data formatting | bytes 5898240 | tf_op jit(solution)/shard_map/while | solution.py:36
  107.2 37.5 %while.10 = (s32[]{:T(128)}, bf16[8,8,32,128]{3,2,1,0:T(8,128)(2,1)}, pred[32,1440]{1,0:T(8,128)(4,1)S(1)}, bf16[8,8,32,128]{3,1,0,2:T(8,128)(2,1)}, bf16[8,1440...) while((s32[]{:T(128)}, bf16[8,8,32,128]{3,2,1,0:T(8,128)(2,1)}, ...), condition=%wide.region_5.6_spmd, body=%wide.region_2.5_spmd.sunk | while | flops 191389184 | bytes 5475921 | solution.py:36
  109.9 2.0 %fusion.37 = bf16[8,8,32,128]{3,2,1,0:T(8,128)(2,1)} fusion(bf16[8,8,32,128]{3,2,1,0:T(8,128)(2,1)} %get-tuple-element.141, s32[]{:T(128)} %get-tuple-element.140, f32[8,32,1440]{2,1,0:T(8,128)S(1)} %get-tuple-element.131, f32[8,32]{1,0:T(8,128)S(1)} %get-tuple-element.132, bf16[8,1440,128]{2,1,0:T(8,128)(2,1)} %get-tuple-element.152, ...), kind=kOutput, calls=%fused_computation.8.clone.1 | convolution fusion | flops 95174656 | bytes 1911808 | tf_op jit(solution)/shard_map/while/body/eval_jaxpr/gsk,kd->gsd/dot_general | solution.py:33
  114.6 2.0 %fusion.37 = bf16[8,8,32,128]{3,2,1,0:T(8,128)(2,1)} fusion(bf16[8,8,32,128]{3,2,1,0:T(8,128)(2,1)} %get-tuple-element.141, s32[]{:T(128)} %get-tuple-element.140, f32[8,32,1440]{2,1,0:T(8,128)S(1)} %get-tuple-element.131, f32[8,32]{1,0:T(8,128)S(1)} %get-tuple-element.132, bf16[8,1440,128]{2,1,0:T(8,128)(2,1)} %get-tuple-element.152, ...), kind=kOutput, calls=%fused_computation.8.clone.1 | convolution fusion | flops 95174656 | bytes 1911808 | tf_op jit(solution)/shard_map/while/body/eval_jaxpr/gsk,kd->gsd/dot_general | solution.py:33
  119.2 2.0 %fusion.37 = bf16[8,8,32,128]{3,2,1,0:T(8,128)(2,1)} fusion(bf16[8,8,32,128]{3,2,1,0:T(8,128)(2,1)} %get-tuple-element.141, s32[]{:T(128)} %get-tuple-element.140, f32[8,32,1440]{2,1,0:T(8,128)S(1)} %get-tuple-element.131, f32[8,32]{1,0:T(8,128)S(1)} %get-tuple-element.132, bf16[8,1440,128]{2,1,0:T(8,128)(2,1)} %get-tuple-element.152, ...), kind=kOutput, calls=%fused_computation.8.clone.1 | convolution fusion | flops 95174656 | bytes 1911808 | tf_op jit(solution)/shard_map/while/body/eval_jaxpr/gsk,kd->gsd/dot_general | solution.py:33
  123.9 2.0 %fusion.37 = bf16[8,8,32,128]{3,2,1,0:T(8,128)(2,1)} fusion(bf16[8,8,32,128]{3,2,1,0:T(8,128)(2,1)} %get-tuple-element.141, s32[]{:T(128)} %get-tuple-element.140, f32[8,32,1440]{2,1,0:T(8,128)S(1)} %get-tuple-element.131, f32[8,32]{1,0:T(8,128)S(1)} %get-tuple-element.132, bf16[8,1440,128]{2,1,0:T(8,128)(2,1)} %get-tuple-element.152, ...), kind=kOutput, calls=%fused_computation.8.clone.1 | convolution fusion | flops 95174656 | bytes 1911808 | tf_op jit(solution)/shard_map/while/body/eval_jaxpr/gsk,kd->gsd/dot_general | solution.py:33
  128.6 2.0 %fusion.37 = bf16[8,8,32,128]{3,2,1,0:T(8,128)(2,1)} fusion(bf16[8,8,32,128]{3,2,1,0:T(8,128)(2,1)} %get-tuple-element.141, s32[]{:T(128)} %get-tuple-element.140, f32[8,32,1440]{2,1,0:T(8,128)S(1)} %get-tuple-element.131, f32[8,32]{1,0:T(8,128)S(1)} %get-tuple-element.132, bf16[8,1440,128]{2,1,0:T(8,128)(2,1)} %get-tuple-element.152, ...), kind=kOutput, calls=%fused_computation.8.clone.1 | convolution fusion | flops 95174656 | bytes 1911808 | tf_op jit(solution)/shard_map/while/body/eval_jaxpr/gsk,kd->gsd/dot_general | solution.py:33
  146.1 23.2 %all_to_all.32 = bf16[16,2,8192]{2,1,0:T(2,128)(2,1)S(1)} all-to-all(bf16[16,2,8192]{2,1,0:T(2,128)(2,1)S(1)} %reshape_reshape.7), channel_id=1, replica_groups=mesh['groups'=2,'branch'=16] {'branch'}, dimensions={0} | all-to-all | bytes 1048576 | tf_op jit(solution)/shard_map/all_to_all | solution.py:120
  (72 shorter events, 46.8 us)
Async XLA Ops:
  0.0 31.1 %copy-start = (bf16[16,8192]{1,0:T(8,128)(2,1)S(1)}, bf16[16,8192]{1,0:T(8,128)(2,1)}, u32[]{:S(2)}) copy-start(bf16[16,8192]{1,0:T(8,128)(2,1)} %param.17) | copy-start | bytes 786436
  0.0 42.5 %copy-start.2 = (s32[1,16]{1,0:T(1,128)S(1)}, s32[1,16]{1,0:T(1,128)}, u32[]{:S(2)}) copy-start(s32[1,16]{1,0:T(1,128)} %param.16) | copy-start | bytes 196
  0.0 42.5 %copy-start.1 = (bf16[2,24,2048]{2,1,0:T(8,128)(2,1)S(1)}, bf16[2,24,2048]{2,1,0:T(8,128)(2,1)}, u32[]{:S(2)}) copy-start(bf16[2,24,2048]{2,1,0:T(8,128)(2,1)} %param.14) | copy-start | bytes 589828
  3.9 13.8 %all-to-all-start = ((s32[16,1,1]{2,1,0:T(1,128)}), s32[16,1,1]{2,1,0:T(1,128)S(1)}, u32[]{:S(2)}, u32[]{:S(2)}) async-start(s32[16,1,1]{2,1,0:T(1,128)} %copy.54), calls=%async_computation | async-start | bytes 16384 | tf_op jit(solution)/shard_map/all_to_all | solution.py:92
  17.7 9.9 %all-to-all-start.1 = ((s32[16,1,2]{2,1,0:T(1,128)}), s32[16,1,2]{2,1,0:T(1,128)S(1)}, u32[]{:S(2)}, u32[]{:S(2)}) async-start(s32[16,1,2]{2,1,0:T(1,128)} %bitcast.13), calls=%async_computation.1 | async-start | bytes 16384 | tf_op jit(solution)/shard_map/all_to_all | solution.py:87
  27.6 11.4 %all-to-all-start.4 = ((bf16[16,2,2048]{2,1,0:T(2,128)(2,1)}), bf16[16,2,2048]{2,1,0:T(2,128)(2,1)S(1)}, u32[]{:S(2)}, u32[]{:S(2)}) async-start(bf16[16,2,2048]{2,1,0:T(2,128)(2,1)} %reshape.133), calls=%async_computation.4 | async-start | bytes 262144 | tf_op jit(solution)/shard_map/all_to_all | solution.py:86
  39.0 17.8 %all-to-all-start.2 = ((bf16[16,2,8192]{2,1,0:T(2,128)(2,1)}), bf16[16,2,8192]{2,1,0:T(2,128)(2,1)S(1)}, u32[]{:S(2)}, u32[]{:S(2)}) async-start(bf16[16,2,8192]{2,1,0:T(2,128)(2,1)} %reshape.131), calls=%async_computation.2 | async-start | bytes 1048576 | tf_op jit(solution)/shard_map/all_to_all | solution.py:85
  56.8 35.9 %all-to-all-start.3 = ((bf16[16,24,2048]{2,1,0:T(8,128)(2,1)}), bf16[16,24,2048]{2,1,0:T(8,128)(2,1)S(1)}, u32[]{:S(2)}, u32[]{:S(2)}) async-start(bf16[16,24,2048]{2,1,0:T(8,128)(2,1)} %select_select_fusion), calls=%async_computation.3 | async-start | bytes 3145728 | tf_op jit(solution)/shard_map/all_to_all | solution.py:91
  64.8 4.0 %copy-start.3 = (s32[1,8]{1,0:T(1,128)S(1)}, s32[1,8]{1,0:T(1,128)}, u32[]{:S(2)}) copy-start(s32[1,8]{1,0:T(1,128)} %param.13) | copy-start | bytes 100
where the time goes:
time: 172 us; the launch traced here: 170 us
  waiting for transfers between devices  47.8 us (28%)
  local copies, waits for them, and re-layouts  34 us (20%)
  matrix products  30.3 us (18%)
  blocking collectives  23.2 us (13%)
  starting transfers between devices  22 us (13%)
  other arithmetic  12.9 us (8%)
    all_to_all x1, blocking collectives, body(): lax.all_to_all(outputs.reshape(branches, capacity, -1), 'branch', split_a...  23.2 us
    all_to_all x1, waiting for transfers between devices, body(): lax.all_to_all(outgoing, 'branch', split_axis=0, concat_axis=0, tiled=True)  20.2 us
    dot_general x8, matrix products, one_head(): jnp.einsum('gsk,kd->gsd', probs, value_group, preferred_element_type=jnp....  16.3 us
    all_to_all x1, waiting for transfers between devices, body(): lax.all_to_all(send_q, 'branch', split_axis=0, concat_axis=0, tiled=True)  12.8 us
    dot_general x8, matrix products, one_head(): jnp.einsum('gsd,kd->gsk', query_group, key_group, preferred_element_type=...  11.5 us
    unnamed x10, local copies, waits for them, and re-layouts  7.9 us
    all_to_all x1, starting transfers between devices, body(): lax.all_to_all(outgoing_len, 'branch', split_axis=0, concat_axis=0, tiled...  7.42 us
    dynamic_slice x8, local copies, waits for them, and re-layouts, attend(): heads = lax.map(one_head, (grouped, key_heads, value_heads))  6.75 us
  transfers between devices with their start and end apart: 5, of which 5 were waited for; matrix products, arithmetic and copies ran while one was open for 11% of the time, Pallas kernels for 0%

commit v1 on v0

v1 whole, which is shorter than its diff:
```python
import functools
import math

import jax
import jax.numpy as jnp
from jax import lax
from jax.experimental import pallas as pl
from jax.experimental.pallas import tpu as pltpu
from jax.sharding import PartitionSpec as P

HD = 128
GRP = 8
NEG = -1e30
MESH = pl.DeviceIdType.MESH


def kernel(
    n, across, cap, rlen, res, heads,
    row_of, slot_of, q_ref, kv_ref, meta_ref, pbias_ref, shared_ref, pk_hbm, pv_hbm,
    out_ref,
    pk, pv, xs, xr, mr, gath, tail, kslot, uni, acc, stat, ox, orx,
    psem, lsem, xsend, xrecv, msend, mrecv, gsend, grecv, rsend, rrecv,
):
    me = lax.axis_index("branch")
    kvh = heads // GRP
    pairs = kvh // 2
    width = n * cap
    rows = width * GRP
    kvw = kvh * HD
    line = n // (2 * across)
    core = lax.rem(me, 2)
    chip = me // 2
    y = lax.rem(chip, across)
    z = chip // across
    sibling = me + 1 - 2 * core
    tail_n = tail.shape[0]
    scale = math.log2(math.e) / math.sqrt(HD)

    copy_k = pltpu.make_async_copy(pk_hbm.at[0], pk, psem.at[0])
    copy_v = pltpu.make_async_copy(pv_hbm.at[0], pv, psem.at[1])
    copy_k.start()
    copy_v.start()

    barrier = pltpu.get_barrier_semaphore()

    def greet(i, c):
        pl.semaphore_signal(
            barrier, inc=1, device_id={"branch": lax.rem(me + i, n)}, device_id_type=MESH
        )
        return c

    lax.fori_loop(1, n, greet, 0)

    def place(j, c):
        row = row_of[j]
        xs[j, :heads] = q_ref[row]
        xs[j, heads:] = kv_ref[row]
        return c

    lax.fori_loop(0, width, place, 0)
    pl.semaphore_wait(barrier, n - 1)

    def ship(src, source, e, target, way):
        return pltpu.make_async_remote_copy(
            src_ref=src,
            dst_ref=gath.at[source, e],
            send_sem=gsend.at[way, source * res + e],
            recv_sem=grecv.at[source * res + e],
            device_id={"branch": target},
            device_id_type=MESH,
        )

    def member(zz, yy, cc):
        return (zz * across + yy) * 2 + cc

    def spread(zs, e, first, act):
        source = member(zs, y, core)
        src = shared_ref.at[e] if first else gath.at[source, e]

        @pl.when(jnp.logical_and(zs <= z, z + 1 < line))
        def _():
            act(ship(src, source, e, member(lax.rem(z + 1, line), y, core), 0))

        @pl.when(jnp.logical_and(zs >= z, z >= 1))
        def _():
            act(ship(src, source, e, member(lax.rem(z + line - 1, line), y, core), 1))

        for d in range(1, across):
            act(ship(src, source, e, member(z, lax.rem(y + d, across), core), 1 + d))
        act(ship(src, source, e, sibling, 1 + across))

    def arrived(source, e):
        ship(gath.at[source, e], source, e, sibling, 0).wait_recv()

    begin = lambda copy: copy.start()
    finish = lambda copy: copy.wait_send()

    def on_line(t, act, waits):
        for up in (0, 1):
            zs = z - t if up == 0 else z + t
            ok = zs >= 0 if up == 0 else zs < line

            @pl.when(ok)
            def _():
                zc = lax.rem(zs + line, line)
                for e in range(res):
                    if waits:
                        arrived(member(zc, y, core), e)
                    spread(zc, e, False, act)

    def cross(zs, act, waits):
        for d in range(1, across):
            source = member(zs, lax.rem(y + d, across), core)
            for e in range(res):
                if waits:
                    arrived(source, e)
                act(ship(gath.at[source, e], source, e, sibling, 1 + across))

    def off_line(t, act, waits):
        @pl.when(z - t >= 0)
        def _():
            cross(lax.rem(z - t + line, line), act, waits)

        @pl.when(jnp.logical_and(z + t < line, t > 0))
        def _():
            cross(lax.rem(z + t, line), act, waits)

    def relay(t, c):
        on_line(t, begin, True)
        off_line(t - 1, begin, True)
        return c

    for e in range(res):
        spread(z, e, True, begin)

    def part(ref, b):
        return ref.at[pl.ds(b * cap, cap)]

    def x_copy(i, b, at):
        return pltpu.make_async_remote_copy(
            src_ref=part(xs, b), dst_ref=part(xr, at), send_sem=xsend.at[i], recv_sem=xrecv.at[i],
            device_id={"branch": b}, device_id_type=MESH,
        )

    def m_copy(i, b, at):
        return pltpu.make_async_remote_copy(
            src_ref=meta_ref.at[b], dst_ref=mr.at[at], send_sem=msend.at[i], recv_sem=mrecv.at[i],
            device_id={"branch": b}, device_id_type=MESH,
        )

    def send_x(i, c):
        b = lax.rem(me + i, n)
        x_copy(i, b, me).start()
        m_copy(i, b, me).start()
        return c

    lax.fori_loop(1, n, send_x, 0)
    own_x = pltpu.make_async_copy(part(xs, me), part(xr, me), lsem.at[0])
    own_m = pltpu.make_async_copy(meta_ref.at[me], mr.at[me], lsem.at[1])
    own_x.start()
    own_m.start()
    gath[me] = shared_ref[...]
    tail[...] = jnp.zeros_like(tail)

    def take_x(i, c):
        b = lax.rem(me + n - i, n)
        x_copy(i, b, b).wait_recv()
        m_copy(i, b, b).wait_recv()
        return c

    lax.fori_loop(1, n, take_x, 0)
    own_x.wait()
    own_m.wait()
    copy_k.wait()
    copy_v.wait()

    def queries(p):
        both = xr[:, pl.ds(p * 2 * GRP, 2 * GRP), :].astype(jnp.float32)
        return [
            both[:, k * GRP : (k + 1) * GRP].reshape(rows, HD).astype(jnp.bfloat16)
            for k in range(2)
        ]

    def scores(q, k):
        return lax.dot_general(q, k, (((1,), (1,)), ((), ())), preferred_element_type=jnp.float32)

    half = lax.broadcasted_iota(jnp.int32, (rows, HD), 1) < HD // 2

    def prompt_pair(p):
        for k, q in enumerate(queries(p)):
            h = 2 * p + k
            cols = slice(h * HD, (h + 1) * HD)
            s = scores(q, pk[:, cols]) * scale + pbias_ref[...]
            m = jnp.max(s, axis=-1, keepdims=True)
            w = jnp.exp2(s - m)
            stat[h] = jnp.where(half, m, jnp.sum(w, axis=-1, keepdims=True))
            acc[h] = jnp.dot(
                w.astype(jnp.bfloat16), pv[:, cols], preferred_element_type=jnp.float32
            )

    cuts = [1 + (line - 1) * p // pairs for p in range(pairs + 1)]
    for p in range(pairs):
        prompt_pair(p)
        if cuts[p] < cuts[p + 1]:
            lax.fori_loop(cuts[p], cuts[p + 1], relay, 0)
    off_line(line - 1, begin, True)

    uni[...] = xr[:, heads:, :].astype(jnp.float32).reshape(width * 2 * kvh, HD)
    for j in range(2 * kvh):
        tail[n * rlen : n * rlen + width, j * HD : (j + 1) * HD] = uni[
            pl.ds(j, width, stride=2 * kvh), :
        ].astype(jnp.bfloat16)
    col = lax.broadcasted_iota(jnp.int32, (1, tail_n), 1)

    def limits(s, carry):
        length, live = carry
        meta = mr[s]
        length = jnp.where(col // rlen == s, meta[1:2, 0:1], length)
        for k in range(cap):
            live = jnp.where(col == n * rlen + s * cap + k, meta[2 + k : 3 + k, 0:1], live)
        return length, live

    zero = jnp.zeros((1, tail_n), jnp.int32)
    length, live = lax.fori_loop(0, n, limits, (zero, zero))
    shared_ok = jnp.logical_and(col < n * rlen, lax.rem(col, rlen) < length)
    kslot[...] = jnp.where(shared_ok, -1, jnp.where(live > 0, col - n * rlen, width))
    row_slot = lax.broadcasted_iota(jnp.int32, (rows, 1), 0) // GRP

    def far(i, c):
        for yy in range(across):
            source = member(i, yy, 1 - core)
            for e in range(res):
                arrived(source, e)
        return c

    lax.fori_loop(0, line, far, 0)

    def choose(t, c):
        two = []
        for s in (2 * t, 2 * t + 1):
            pick = mr[s][0:1, 0:1]
            chosen = gath[s, 0].astype(jnp.float32)
            for e in range(1, res):
                chosen = jnp.where(pick == e, gath[s, e].astype(jnp.float32), chosen)
            two.append(chosen)
        tail[pl.ds(pl.multiple_of(t * 2 * rlen, 16), 2 * rlen), :] = jnp.concatenate(
            two, axis=0
        ).astype(jnp.bfloat16)
        return c

    lax.fori_loop(0, n // 2, choose, 0)

    def tail_pair(p):
        done = []
        for k, q in enumerate(queries(p)):
            h = 2 * p + k
            keys = tail[:, h * HD : (h + 1) * HD]
            values = tail[:, kvw + h * HD : kvw + (h + 1) * HD]
            s = jnp.where(kslot[...] <= row_slot, scores(q, keys) * scale, NEG)
            before = stat[h][:, :1]
            m = jnp.maximum(before, jnp.max(s, axis=-1, keepdims=True))
            w = jnp.exp2(s - m)
            keep = jnp.exp2(before - m)
            total = stat[h][:, HD // 2 : HD // 2 + 1] * keep + jnp.sum(w, axis=-1, keepdims=True)
            mixed = acc[h] * keep + jnp.dot(
                w.astype(jnp.bfloat16), values, preferred_element_type=jnp.float32
            )
            done.append((mixed / total).reshape(width, GRP, HD))
        ox[:, p * 2 * GRP : (p + 1) * 2 * GRP, :] = jnp.concatenate(done, axis=1).astype(
            jnp.bfloat16
        )

    def r_copy(p, i, b, at):
        cut = pl.ds(p * 2 * GRP, 2 * GRP)
        return pltpu.make_async_remote_copy(
            src_ref=ox.at[pl.ds(b * cap, cap), cut], dst_ref=orx.at[pl.ds(at * cap, cap), cut],
            send_sem=rsend.at[p, i], recv_sem=rrecv.at[p, i],
            device_id={"branch": b}, device_id_type=MESH,
        )

    def give_back(p):
        def one(i, c):
            r_copy(p, i, lax.rem(me + i, n), me).start()
            return c

        lax.fori_loop(1, n, one, 0)

    for p in range(pairs):
        tail_pair(p)
        if p:
            give_back(p - 1)
    give_back(pairs - 1)
    own_r = pltpu.make_async_copy(part(ox, me), part(orx, me), lsem.at[2])
    own_r.start()

    def sent(i, c):
        b = lax.rem(me + i, n)
        x_copy(i, b, me).wait_send()
        m_copy(i, b, me).wait_send()
        return c

    lax.fori_loop(1, n, sent, 0)
    for e in range(res):
        spread(z, e, True, finish)

    def relayed(t, c):
        on_line(t, finish, False)
        off_line(t - 1, finish, False)
        return c

    lax.fori_loop(1, line, relayed, 0)
    off_line(line - 1, finish, False)

    def returned(i, c):
        for p in range(pairs):
            r_copy(p, i, lax.rem(me + n - i, n), lax.rem(me + n - i, n)).wait_recv()
        return c

    lax.fori_loop(1, n, returned, 0)
    own_r.wait()

    def collect(j, c):
        out_ref[j] = orx[slot_of[j]]
        return c

    lax.fori_loop(0, out_ref.shape[0], collect, 0)

    def gone(i, c):
        for p in range(pairs):
            r_copy(p, i, lax.rem(me + i, n), me).wait_send()
        return c

    lax.fori_loop(1, n, gone, 0)


def body(
    across, prompt_k, prompt_v, prompt_mask, shared_kv, shared_len, send_pick,
    unique_q, unique_kv, unique_owner,
):
    n = lax.axis_size("branch")
    rows = unique_q.shape[0]
    cap = 2 * rows // n
    width = n * cap
    res, rlen = shared_kv.shape[:2]
    heads = unique_q.shape[1] // HD
    kvh = unique_kv.shape[1] // (2 * HD)
    plen = prompt_k.shape[1]
    owner = unique_owner[:, 0]
    order = jnp.arange(rows, dtype=jnp.int32)
    earlier = (owner[:, None] == owner[None, :]) & (order[None, :] < order[:, None])
    slot_of = owner * cap + jnp.sum(earlier.astype(jnp.int32), axis=1)
    matches = jnp.arange(width, dtype=jnp.int32)[:, None] == slot_of[None, :]
    row_of = jnp.sum(jnp.where(matches, order[None, :], 0), axis=1)
    live = jnp.any(matches, axis=1).astype(jnp.int32).reshape(n, cap)
    pick = send_pick[0]
    length = jnp.zeros_like(pick)
    for e in range(res):
        length = jnp.where(pick == e, shared_len[e], length)
    meta = jnp.concatenate([pick[:, None], length[:, None], live], axis=1)
    meta = jnp.broadcast_to(meta[:, :, None], meta.shape + (HD,))
    block = plen // prompt_mask.shape[1]
    pbias = jnp.where(jnp.repeat(prompt_mask > 0, block, axis=1), 0.0, NEG).astype(jnp.float32)
    tail_n = -(-(n * rlen + width) // 128) * 128
    qrows = width * GRP
    vmem = pl.BlockSpec(memory_space=pltpu.VMEM)
    smem = pl.BlockSpec(memory_space=pltpu.SMEM)
    anyp = pl.BlockSpec(memory_space=pl.ANY)
    bf, f32 = jnp.bfloat16, jnp.float32
    dma = pltpu.SemaphoreType.DMA
    out = pl.pallas_call(
        functools.partial(kernel, n, across, cap, rlen, res, heads),
        out_shape=jax.ShapeDtypeStruct((rows, heads, HD), bf),
        in_specs=[smem, smem, vmem, vmem, vmem, vmem, vmem, anyp, anyp],
        out_specs=vmem,
        scratch_shapes=[
            pltpu.VMEM(prompt_k.shape[1:], bf),
            pltpu.VMEM(prompt_v.shape[1:], bf),
            pltpu.VMEM((width, heads + 2 * kvh, HD), bf),
            pltpu.VMEM((width, heads + 2 * kvh, HD), bf),
            pltpu.VMEM((n,) + meta.shape[1:], jnp.int32),
            pltpu.VMEM((n,) + shared_kv.shape, bf),
            pltpu.VMEM((tail_n, 2 * kvh * HD), bf),
            pltpu.VMEM((1, tail_n), jnp.int32),
            pltpu.VMEM((width * 2 * kvh, HD), f32),
            pltpu.VMEM((kvh, qrows, HD), f32),
            pltpu.VMEM((kvh, qrows, HD), f32),
            pltpu.VMEM((width, heads, HD), bf),
            pltpu.VMEM((width, heads, HD), bf),
            dma((2,)),
            dma((3,)),
            dma((n,)),
            dma((n,)),
            dma((n,)),
            dma((n,)),
            dma((2 + across, n * res)),
            dma((n * res,)),
            dma((kvh // 2, n)),
            dma((kvh // 2, n)),
        ],
        compiler_params=pltpu.CompilerParams(
            collective_id=0, has_side_effects=True, vmem_limit_bytes=62 * 1024 * 1024
        ),
    )(
        row_of, slot_of, unique_q.reshape(rows, heads, HD),
        unique_kv.reshape(rows, 2 * kvh, HD), meta, pbias, shared_kv, prompt_k, prompt_v,
    )
    return out.reshape(rows, heads * HD)


def chips_across(mesh):
    devices = mesh.devices.reshape(-1, mesh.shape["branch"])[0]
    try:
        places = [tuple(d.coords) for d in devices[::2]]
    except (AttributeError, TypeError):
        return 1
    return sum(1 for p in places if p[2] == places[0][2])


def solution(mesh):
    spec1, spec2, spec3 = (P(("groups", "branch"), *(None,) * k) for k in range(3))
    in_specs = (spec3, spec3, spec2, spec3, spec1, spec2, spec2, spec2, spec2)
    return jax.shard_map(
        functools.partial(body, chips_across(mesh)),
        mesh=mesh, in_specs=in_specs, out_specs=spec2, check_vma=False,
    )
```

time: 172 us -> 77.5 us (0.45)
  Pallas kernels: 0 us -> 63.6 us
  waiting for transfers between devices: 47.8 us -> 0 us
  matrix products: 30.3 us -> 0 us
  local copies, waits for them, and re-layouts: 34 us -> 8.57 us
  blocking collectives: 23.2 us -> 0 us
  starting transfers between devices: 22 us -> 0 us
  other arithmetic: 12.9 us -> 5.03 us
    pallas_call x0 -> x1, Pallas kernels: none -> 63.6 us  [body(): pl.pallas_call(functools.partial(kernel, n, across, cap, rlen, res, heads...]
    all_to_all x5 -> x0, waiting for transfers between devices: 47.8 us -> none  [the longest x1 20.2 us: body(): lax.all_to_all(outgoing, 'branch', split_axis=0, concat_axis=0, tiled=True)]
    dot_general x19 -> x0, matrix products: 30.3 us -> none  [the longest x8 16.3 us: one_head(): jnp.einsum('gsk,kd->gsd', probs, value_group, preferred_element_type=jnp....]
    all_to_all x1 -> x0, blocking collectives: 23.2 us -> none  [body(): lax.all_to_all(outputs.reshape(branches, capacity, -1), 'branch', split_a...]
    all_to_all x5 -> x0, starting transfers between devices: 22 us -> none  [the longest x1 7.42 us: body(): lax.all_to_all(outgoing_len, 'branch', split_axis=0, concat_axis=0, tiled...]
    dynamic_slice x8 -> x0, local copies, waits for them, and re-layouts: 6.75 us -> none  [attend(): heads = lax.map(one_head, (grouped, key_heads, value_heads))]
    while x2 -> x0, local copies, waits for them, and re-layouts: 5.53 us -> none  [attend(): heads = lax.map(one_head, (grouped, key_heads, value_heads))]
    slice x5 -> x1, local copies, waits for them, and re-layouts: 5.83 us -> 1.32 us  [body(): length = jnp.where(pick == e, shared_len[e], length)]
  transfers between devices with their start and end apart: 5 -> 0, of which waited for: 5 -> 0; matrix products, arithmetic and copies ran while one was open for 11% -> 0% of each run, Pallas kernels for 0% -> 0%
where the time goes in v1:
time: 77.5 us; the launch traced here: 77.2 us
  Pallas kernels  63.6 us (82%)
  local copies, waits for them, and re-layouts  8.57 us (11%)
  other arithmetic  5.03 us (6%)
    pallas_call x1, Pallas kernels, body(): pl.pallas_call(functools.partial(kernel, n, across, cap, rlen, res, heads...  63.6 us
    unnamed x5, local copies, waits for them, and re-layouts  5 us
    select_n x1, other arithmetic, body(): length = jnp.where(pick == e, shared_len[e], length)  1.99 us

profile of v1, /device:TPU:0, one launch (start us, length us, event | category | flops | bytes accessed | tf_op | source)
XLA Modules:
  0.0 77.2 jit_solution(284850807034589438)
XLA Ops:
  0.0 0.7 fusion.2
  0.7 0.9 %convert_reduce_fusion = s32[16]{0:T(128)S(1)} fusion(s32[16]{0:T(128)} %bitcast.24), kind=kLoop, calls=%fused_computation.3 | loop fusion | flops 1264 | bytes 128 | tf_op jit(solution)/shard_map/reduce_sum | solution.py:351
  1.6 0.7 multiply_add_fusion.slot_of
  2.2 0.0 copy-start
  2.2 0.1 fusion
  2.3 0.6 select_reduce_fusion.row_of
  3.0 1.3 %fusion.3 = (s32[1]{0:T(128)}, s32[1]{0:T(128)}) fusion(s32[2]{0:T(128)} %param.13), kind=kLoop, calls=%fused_computation.13 | loop fusion | bytes 16 | tf_op jit(solution)/shard_map/slice | solution.py:358
  4.3 2.0 %compare_select_fusion.2 = s32[16,1]{0,1:T(1,128)S(1)} fusion(s32[]{:T(128)} %bitcast.3, s32[]{:T(128)} %bitcast.2, s32[1,16]{1,0:T(1,128)} %param.14), kind=kLoop, calls=%fused_computation.10 | loop fusion | flops 64 | bytes 136 | tf_op jit(solution)/shard_map/jit(_where)/select_n | solution.py:358
  6.3 0.7 broadcast_in_dim.49
  6.9 0.1 copy.17
  7.0 0.1 reshape.74
  7.1 0.7 copy.16
  7.8 0.1 pad_add_fusion
  7.9 0.7 broadcast_in_dim.46.meta_ref
  8.6 1.5 %copy.19 = bf16[2,8,16,128]{3,2,1,0:T(8,128)(2,1)} copy(bf16[2,8,16,128]{3,1,2,0:T(8,128)(2,1)} %bitcast.21) | data formatting | bytes 131072
  10.1 1.7 %copy.18 = bf16[2,8,64,128]{3,2,1,0:T(8,128)(2,1)} copy(bf16[2,8,64,128]{3,1,2,0:T(8,128)(2,1)} %bitcast.20) | data formatting | bytes 524288
  11.8 0.0 copy-done
  11.8 63.6 %shard_map.91 = bf16[16,64,128]{2,1,0:T(8,128)(2,1)} custom-call(s32[32]{0:T(128)} %select_reduce_fusion.row_of, s32[16]{0:T(128)} %copy-done, bf16[16,64,128]{2,1,0:T(8,128)(2,1)} %bitcast.18, bf16[16,16,128]{2,1,0:T(8,128)(2,1)} %bitcast.19, s32[16,4,128]{2,1,0:T(4,128)} %broadcast_in_dim.46.meta_ref, f32[1,1024]{1,0:T(1,128)} %bitcast.22, ...), custom_call_target="tpu_custom_call" | custom-call | tf_op jit(solution)/shard_map/pallas_call | solution.py:370
  75.4 1.8 %copy.22 = bf16[2,8,64,128]{3,1,2,0:T(8,128)(2,1)} copy(bf16[2,8,64,128]{3,2,1,0:T(8,128)(2,1)} %bitcast.17) | data formatting | bytes 524288
  (1 shorter events, 0.0 us)
Async XLA Ops:
  2.2 9.5 %copy-start = (s32[16]{0:T(128)}, s32[16]{0:T(128)S(1)}, u32[]{:S(2)}) copy-start(s32[16]{0:T(128)S(1)} %multiply_add_fusion.slot_of) | copy-start | bytes 196

commit v2 on v1

--- a/solution.py
+++ b/solution.py
@@ -16,9 +16,9 @@
 
 def kernel(
     n, across, cap, rlen, res, heads,
-    row_of, slot_of, q_ref, kv_ref, meta_ref, pbias_ref, shared_ref, pk_hbm, pv_hbm,
+    owner_ref, pick_ref, len_ref, mask_ref, q_ref, kv_ref, shared_ref, pk_hbm, pv_hbm,
     out_ref,
-    pk, pv, xs, xr, mr, gath, tail, kslot, uni, acc, stat, ox, orx,
+    pk, pv, flat, by_row, slot_of, pbias, meta_ref, xs, xr, mr, gath, tail, kslot, acc, stat, ox, orx,
     psem, lsem, xsend, xrecv, msend, mrecv, gsend, grecv, rsend, rrecv,
 ):
     me = lax.axis_index("branch")
@@ -51,13 +51,58 @@
 
     lax.fori_loop(1, n, greet, 0)
 
-    def place(j, c):
-        row = row_of[j]
-        xs[j, :heads] = q_ref[row]
-        xs[j, heads:] = kv_ref[row]
-        return c
-
-    lax.fori_loop(0, width, place, 0)
+    count = q_ref.shape[0]
+    per = heads + 2 * kvh
+    some = min(count, 16)
+    for r in range(0, count, some):
+        for h in range(per):
+            ref, g = (q_ref, h) if h < heads else (kv_ref, h - heads)
+            flat[pl.ds(h, some, stride=per), :] = ref[
+                r : r + some, g * HD : (g + 1) * HD
+            ].astype(jnp.float32)
+        for i in range(some):
+            by_row[r + i] = flat[i * per : (i + 1) * per].astype(jnp.bfloat16)
+
+    def number(j, c):
+        mine = owner_ref[j]
+        rank = lax.fori_loop(
+            0, j, lambda i, r: r + jnp.where(owner_ref[i] == mine, 1, 0), jnp.int32(0)
+        )
+        slot_of[j] = mine * cap + rank
+        return c
+
+    lax.fori_loop(0, count, number, 0)
+
+    def place(b, c):
+        def scan(i, found):
+            hit = owner_ref[i] == b
+            rows_at, seen = found[:cap], found[cap]
+            rows_at = [
+                jnp.where(jnp.logical_and(hit, seen == k), i, r) for k, r in enumerate(rows_at)
+            ]
+            return (*rows_at, seen + jnp.where(hit, 1, 0))
+
+        found = lax.fori_loop(0, count, scan, (jnp.int32(0),) * (cap + 1))
+        pick = pick_ref[0, b]
+        length = jnp.int32(0)
+        for e in range(res):
+            length = jnp.where(pick == e, len_ref[e], length)
+        meta_ref[b, 0:1] = jnp.full((1, HD), pick, jnp.int32)
+        meta_ref[b, 1:2] = jnp.full((1, HD), length, jnp.int32)
+        for k in range(cap):
+            xs[b * cap + k] = by_row[found[k]]
+            meta_ref[b, 2 + k : 3 + k] = jnp.full(
+                (1, HD), jnp.where(found[cap] > k, 1, 0), jnp.int32
+            )
+        return c
+
+    lax.fori_loop(0, n, place, 0)
+    blocks = mask_ref.shape[1]
+    block = pk.shape[0] // blocks
+    for g in range(blocks):
+        pbias[:, g * block : (g + 1) * block] = jnp.full(
+            (1, block), jnp.where(mask_ref[0, g] > 0, 0.0, NEG), jnp.float32
+        )
     pl.semaphore_wait(barrier, n - 1)
 
     def ship(src, source, e, target, way):
@@ -130,8 +175,6 @@
         off_line(t - 1, begin, True)
         return c
 
-    for e in range(res):
-        spread(z, e, True, begin)
 
     def part(ref, b):
         return ref.at[pl.ds(b * cap, cap)]
@@ -155,6 +198,8 @@
         return c
 
     lax.fori_loop(1, n, send_x, 0)
+    for e in range(res):
+        spread(z, e, True, begin)
     own_x = pltpu.make_async_copy(part(xs, me), part(xr, me), lsem.at[0])
     own_m = pltpu.make_async_copy(meta_ref.at[me], mr.at[me], lsem.at[1])
     own_x.start()
@@ -190,7 +235,7 @@
         for k, q in enumerate(queries(p)):
             h = 2 * p + k
             cols = slice(h * HD, (h + 1) * HD)
-            s = scores(q, pk[:, cols]) * scale + pbias_ref[...]
+            s = scores(q, pk[:, cols]) * scale + pbias[...]
             m = jnp.max(s, axis=-1, keepdims=True)
             w = jnp.exp2(s - m)
             stat[h] = jnp.where(half, m, jnp.sum(w, axis=-1, keepdims=True))
@@ -205,9 +250,11 @@
             lax.fori_loop(cuts[p], cuts[p + 1], relay, 0)
     off_line(line - 1, begin, True)
 
-    uni[...] = xr[:, heads:, :].astype(jnp.float32).reshape(width * 2 * kvh, HD)
+    flat[: width * 2 * kvh] = (
+        xr[:, heads:, :].astype(jnp.float32).reshape(width * 2 * kvh, HD)
+    )
     for j in range(2 * kvh):
-        tail[n * rlen : n * rlen + width, j * HD : (j + 1) * HD] = uni[
+        tail[n * rlen : n * rlen + width, j * HD : (j + 1) * HD] = flat[
             pl.ds(j, width, stride=2 * kvh), :
         ].astype(jnp.bfloat16)
     col = lax.broadcasted_iota(jnp.int32, (1, tail_n), 1)
@@ -319,11 +366,13 @@
     lax.fori_loop(1, n, returned, 0)
     own_r.wait()
 
-    def collect(j, c):
-        out_ref[j] = orx[slot_of[j]]
-        return c
-
-    lax.fori_loop(0, out_ref.shape[0], collect, 0)
+    for r in range(0, count, some):
+        for i in range(some):
+            flat[i * heads : (i + 1) * heads] = orx[slot_of[r + i]].astype(jnp.float32)
+        for h in range(heads):
+            out_ref[r : r + some, h * HD : (h + 1) * HD] = flat[
+                pl.ds(h, some, stride=heads), :
+            ].astype(jnp.bfloat16)
 
     def gone(i, c):
         for p in range(pairs):
@@ -345,21 +394,6 @@
     heads = unique_q.shape[1] // HD
     kvh = unique_kv.shape[1] // (2 * HD)
     plen = prompt_k.shape[1]
-    owner = unique_owner[:, 0]
-    order = jnp.arange(rows, dtype=jnp.int32)
-    earlier = (owner[:, None] == owner[None, :]) & (order[None, :] < order[:, None])
-    slot_of = owner * cap + jnp.sum(earlier.astype(jnp.int32), axis=1)
-    matches = jnp.arange(width, dtype=jnp.int32)[:, None] == slot_of[None, :]
-    row_of = jnp.sum(jnp.where(matches, order[None, :], 0), axis=1)
-    live = jnp.any(matches, axis=1).astype(jnp.int32).reshape(n, cap)
-    pick = send_pick[0]
-    length = jnp.zeros_like(pick)
-    for e in range(res):
-        length = jnp.where(pick == e, shared_len[e], length)
-    meta = jnp.concatenate([pick[:, None], length[:, None], live], axis=1)
-    meta = jnp.broadcast_to(meta[:, :, None], meta.shape + (HD,))
-    block = plen // prompt_mask.shape[1]
-    pbias = jnp.where(jnp.repeat(prompt_mask > 0, block, axis=1), 0.0, NEG).astype(jnp.float32)
     tail_n = -(-(n * rlen + width) // 128) * 128
     qrows = width * GRP
     vmem = pl.BlockSpec(memory_space=pltpu.VMEM)
@@ -369,19 +403,23 @@
     dma = pltpu.SemaphoreType.DMA
     out = pl.pallas_call(
         functools.partial(kernel, n, across, cap, rlen, res, heads),
-        out_shape=jax.ShapeDtypeStruct((rows, heads, HD), bf),
-        in_specs=[smem, smem, vmem, vmem, vmem, vmem, vmem, anyp, anyp],
+        out_shape=jax.ShapeDtypeStruct((rows, heads * HD), bf),
+        in_specs=[smem, smem, smem, smem, vmem, vmem, vmem, anyp, anyp],
         out_specs=vmem,
         scratch_shapes=[
             pltpu.VMEM(prompt_k.shape[1:], bf),
             pltpu.VMEM(prompt_v.shape[1:], bf),
+            pltpu.VMEM((max(min(rows, 16) * (heads + 2 * kvh), width * 2 * kvh), HD), f32),
+            pltpu.VMEM((rows, heads + 2 * kvh, HD), bf),
+            pltpu.SMEM((rows,), jnp.int32),
+            pltpu.VMEM((1, plen), f32),
+            pltpu.VMEM((n, 2 + cap, HD), jnp.int32),
             pltpu.VMEM((width, heads + 2 * kvh, HD), bf),
             pltpu.VMEM((width, heads + 2 * kvh, HD), bf),
-            pltpu.VMEM((n,) + meta.shape[1:], jnp.int32),
+            pltpu.VMEM((n, 2 + cap, HD), jnp.int32),
             pltpu.VMEM((n,) + shared_kv.shape, bf),
             pltpu.VMEM((tail_n, 2 * kvh * HD), bf),
             pltpu.VMEM((1, tail_n), jnp.int32),
-            pltpu.VMEM((width * 2 * kvh, HD), f32),
             pltpu.VMEM((kvh, qrows, HD), f32),
             pltpu.VMEM((kvh, qrows, HD), f32),
             pltpu.VMEM((width, heads, HD), bf),
@@ -398,13 +436,13 @@
             dma((kvh // 2, n)),
         ],
         compiler_params=pltpu.CompilerParams(
-            collective_id=0, has_side_effects=True, vmem_limit_bytes=62 * 1024 * 1024
+            collective_id=0, has_side_effects=True, vmem_limit_bytes=67043328
         ),
     )(
-        row_of, slot_of, unique_q.reshape(rows, heads, HD),
-        unique_kv.reshape(rows, 2 * kvh, HD), meta, pbias, shared_kv, prompt_k, prompt_v,
+        unique_owner.reshape(rows), send_pick, shared_len, prompt_mask,
+        unique_q, unique_kv, shared_kv, prompt_k, prompt_v,
     )
-    return out.reshape(rows, heads * HD)
+    return out
 
 
 def chips_across(mesh):

time: 77.5 us -> 64.8 us (0.84)
  local copies, waits for them, and re-layouts: 8.57 us -> 1.67 us
  other arithmetic: 5.03 us -> 0 us
    unnamed x5 -> x1, local copies, waits for them, and re-layouts: 5 us -> 1.67 us
    select_n x2 -> x0, other arithmetic: 2.65 us -> none  [the longest x1 1.99 us: body(): length = jnp.where(pick == e, shared_len[e], length)]
    reduce_sum x2 -> x0, other arithmetic: 1.54 us -> none  [the longest x1 0.91 us: body(): slot_of = owner * cap + jnp.sum(earlier.astype(jnp.int32), axis=1)]
    broadcast_in_dim x2 -> x0, local copies, waits for them, and re-layouts: 1.35 us -> none  [the longest x1 0.7 us: body(): meta = jnp.broadcast_to(meta[:, :, None], meta.shape + (HD,))]
    slice x1 -> x0, local copies, waits for them, and re-layouts: 1.32 us -> none  [body(): length = jnp.where(pick == e, shared_len[e], length)]
where the time goes in v2:
time: 64.8 us; the launch traced here: 64.6 us
  Pallas kernels  62.9 us (97%)
  local copies, waits for them, and re-layouts  1.67 us (3%)
    pallas_call x1, Pallas kernels, body(): pl.pallas_call(functools.partial(kernel, n, across, cap, rlen, res, heads...  62.9 us
    unnamed x1, local copies, waits for them, and re-layouts  1.67 us

profile of v2, /device:TPU:0, one launch (start us, length us, event | category | flops | bytes accessed | tf_op | source)
XLA Modules:
  0.0 64.6 jit_solution(11649939475300551775)
XLA Ops:
  0.0 62.9 %shard_map.91 = bf16[16,8192]{1,0:T(8,128)(2,1)} custom-call(s32[16]{0:T(128)} %bitcast.1, s32[1,16]{1,0:T(1,128)} %pick_ref.1, s32[2]{0:T(128)} %len_ref.1, s32[1,8]{1,0:T(1,128)} %mask_ref.1, bf16[16,8192]{1,0:T(8,128)(2,1)} %q_ref.1, bf16[16,2048]{1,0:T(8,128)(2,1)} %kv_ref.1, bf16[2,24,2048]{2,1,0:T(8,128)(2,1)} %shared_ref.1, ...), custom_call_target="tpu_custom_call" | custom-call | tf_op jit(solution)/shard_map/pallas_call | solution.py:404
  62.9 1.7 %copy.11 = bf16[16,8192]{1,0:T(8,128)(2,1)} copy(bf16[16,8192]{1,0:T(8,128)(2,1)} %shard_map.91) | data formatting | bytes 524288

commit v3 on v2

--- a/solution.py
+++ b/solution.py
@@ -74,15 +74,19 @@
     lax.fori_loop(0, count, number, 0)
 
     def place(b, c):
-        def scan(i, found):
-            hit = owner_ref[i] == b
-            rows_at, seen = found[:cap], found[cap]
-            rows_at = [
-                jnp.where(jnp.logical_and(hit, seen == k), i, r) for k, r in enumerate(rows_at)
-            ]
-            return (*rows_at, seen + jnp.where(hit, 1, 0))
-
-        found = lax.fori_loop(0, count, scan, (jnp.int32(0),) * (cap + 1))
+        def scan(r, found):
+            for u in range(some):
+                i = r * some + u
+                hit = owner_ref[i] == b
+                rows_at, seen = found[:cap], found[cap]
+                rows_at = [
+                    jnp.where(jnp.logical_and(hit, seen == k), i, at)
+                    for k, at in enumerate(rows_at)
+                ]
+                found = (*rows_at, seen + jnp.where(hit, 1, 0))
+            return found
+
+        found = lax.fori_loop(0, count // some, scan, (jnp.int32(0),) * (cap + 1))
         pick = pick_ref[0, b]
         length = jnp.int32(0)
         for e in range(res):

time: 64.8 us -> 63.9 us (0.986)
  Pallas kernels: 62.9 us -> 62 us
    pallas_call x1, Pallas kernels: 62.9 us -> 62 us  [body(): pl.pallas_call(functools.partial(kernel, n, across, cap, rlen, res, heads...]
where the time goes in v3:
time: 63.9 us; the launch traced here: 63.7 us
  Pallas kernels  62 us (97%)
  local copies, waits for them, and re-layouts  1.67 us (3%)
    pallas_call x1, Pallas kernels, body(): pl.pallas_call(functools.partial(kernel, n, across, cap, rlen, res, heads...  62 us
    unnamed x1, local copies, waits for them, and re-layouts  1.67 us

profile of v3, /device:TPU:0, one launch (start us, length us, event | category | flops | bytes accessed | tf_op | source)
XLA Modules:
  0.0 63.7 jit_solution(15987543220062219334)
XLA Ops:
  0.0 62.0 %shard_map.91 = bf16[16,8192]{1,0:T(8,128)(2,1)} custom-call(s32[16]{0:T(128)} %bitcast.1, s32[1,16]{1,0:T(1,128)} %pick_ref.1, s32[2]{0:T(128)} %len_ref.1, s32[1,8]{1,0:T(1,128)} %mask_ref.1, bf16[16,8192]{1,0:T(8,128)(2,1)} %q_ref.1, bf16[16,2048]{1,0:T(8,128)(2,1)} %kv_ref.1, bf16[2,24,2048]{2,1,0:T(8,128)(2,1)} %shared_ref.1, ...), custom_call_target="tpu_custom_call" | custom-call | tf_op jit(solution)/shard_map/pallas_call | solution.py:408
  62.1 1.7 %copy.11 = bf16[16,8192]{1,0:T(8,128)(2,1)} copy(bf16[16,8192]{1,0:T(8,128)(2,1)} %shard_map.91) | data formatting | bytes 524288
